TPU v7x, 128 devices: a whole 4x4x4 slice. The times are simulated.
128 devices in a mesh: slab: 64 (over z, y, x), tile: 2 (over core).
Axes of the slice: x: 4, y: 4, z: 4, core: 2. Of those that a mesh axis runs over, the one named last changes fastest.
Arguments:
- samples: float32 [64, 256, 32, 256], P('slab', None, 'tile'), may hold values from -6 to 6
- counts: int32 [64, 256, 32], P('slab', None, 'tile'), may hold values from 1 to 4
- w_in: float32 [64, 64, 256], P('slab'), may hold values from -0.75 to 0.75
- b_in: float32 [64, 256], P('slab'), may hold values from -3 to 3
- w_color: float32 [64, 256, 128], P('slab'), may hold values from -0.375 to 0.375
- b_color: float32 [64, 128], P('slab'), may hold values from -3 to 3
- w_density: float32 [64, 256], P('slab'), may hold values from -0.375 to 0.375
- b_density: float32 [64], P('slab'), may hold values from -1 to 1
- conv_a: bfloat16 [3, 3, 128, 128], replicated, may hold values from -0.1875 to 0.1875
- bias_a: float32 [128], replicated, may hold values from -3 to 3
- conv_b: bfloat16 [3, 3, 128, 128], replicated, may hold values from -0.1875 to 0.1875
- bias_b: float32 [128], replicated, may hold values from -3 to 3
Outputs:
- decoded: bfloat16 [256, 32, 128], P('slab', 'tile')
- front: float32 [64, 256, 32], P('slab', None, 'tile')
All inputs are finite; a program needn't handle non-finite values.
Results may differ from a plain program's by a relative error of at most 0.006.
Values may be sent and summed in bfloat16 or wider, within the bound.
No kernel may reach another device: no remote copies, remote signals or barrier semaphores. Data moves between devices by JAX's collectives and lax.ppermute only.
A program may use at most 128 MiB of HBM per device.

v0:
```python
import jax
import jax.numpy as jnp
from jax import lax
from jax.sharding import PartitionSpec as P

F = 64
K = 4


def padded_2(cells, sides, width):
    for axis, dim in sides:
        count = lax.axis_size(axis)
        ends = count - 1
        head = lax.slice_in_dim(cells, 0, width, axis=dim)
        tail = lax.slice_in_dim(cells, cells.shape[dim] - width, cells.shape[dim], axis=dim)
        cells = jnp.concatenate(
            [
                lax.ppermute(tail, axis, [(i, (i + 1) % count) for i in range(ends)]),
                cells,
                lax.ppermute(head, axis, [((i + 1) % count, i) for i in range(ends)]),
            ],
            axis=dim,
        )
    return cells


def prefix_2(part, axis, combine, identity):
    place = lax.axis_index(axis)
    gathered = lax.all_gather(part, axis)
    state = jnp.zeros_like(part) + jnp.asarray(identity, part.dtype)

    def one(turn, state):
        return combine(state, lax.dynamic_index_in_dim(gathered, turn, 0, False))

    return lax.fori_loop(0, place, one, state)


def hidden_units(inputs, w_in, b_in):
    shaped = inputs.reshape(inputs.shape[:-1] + (K, F))
    return jax.nn.relu(
        jnp.einsum("rwkf,fh->rwkh", shaped, w_in, precision=lax.Precision.HIGHEST) + b_in
    )


def densities(hidden_act, w_density, b_density, live_count):
    before = (
        jnp.einsum("rwkh,h->rwk", hidden_act, w_density, precision=lax.Precision.HIGHEST)
        + b_density
    )
    slots = lax.broadcasted_iota(jnp.int32, before.shape, 2)
    return jnp.where(slots < live_count[..., None], jax.nn.softplus(before), 0.0)


def sample_weights(density, front, total):
    scaled = density / total[..., None]
    earlier = jnp.cumsum(scaled, axis=2) - scaled
    return jnp.exp(-front[..., None] - earlier) * (1.0 - jnp.exp(-scaled))


def partial_image(hidden_act, weight, w_color, b_color):
    color = (
        jnp.einsum("rwkh,hc->rwkc", hidden_act, w_color, precision=lax.Precision.HIGHEST) + b_color
    )
    return jnp.einsum("rwk,rwkc->rwc", weight, color, precision=lax.Precision.HIGHEST)


def add_pair(earlier, later):
    return earlier + later


def convolve(padded, kernel, out_rows, out_cols):
    result = jnp.zeros((out_rows, out_cols, kernel.shape[3]), jnp.float32)
    for row_shift in range(3):
        for col_shift in range(3):
            window = padded[row_shift : row_shift + out_rows, col_shift : col_shift + out_cols]
            result = result + jnp.einsum(
                "rwc,cd->rwd",
                window,
                kernel[row_shift, col_shift],
                preferred_element_type=jnp.float32,
            )
    return result


def strip_edges(field):
    return padded_2(field, (("slab", 0), ("tile", 1)), 1)


def body(
    samples,
    counts,
    w_in,
    b_in,
    w_color,
    b_color,
    w_density,
    b_density,
    conv_a,
    bias_a,
    conv_b,
    bias_b,
):
    slab_count = lax.axis_size("slab")
    height = samples.shape[1]
    tile_cols = samples.shape[2]
    strip_rows = height // slab_count
    hidden_act = hidden_units(samples[0], w_in[0], b_in[0])
    density = densities(hidden_act, w_density[0], b_density[0], counts[0])
    depth = jnp.sum(density, axis=2)
    prefix = prefix_2(depth, "slab", add_pair, jnp.zeros_like(depth))
    total = lax.psum(depth, "slab")
    front = prefix / total
    weight = sample_weights(density, front, total)
    image = lax.psum_scatter(
        partial_image(hidden_act, weight, w_color[0], b_color[0]),
        "slab",
        scatter_dimension=0,
        tiled=True,
    ).astype(jnp.bfloat16)
    first_pad = strip_edges(image)
    hidden_map = jax.nn.relu(convolve(first_pad, conv_a, strip_rows, tile_cols) + bias_a).astype(
        jnp.bfloat16
    )
    second_pad = strip_edges(hidden_map)
    decoded = (convolve(second_pad, conv_b, strip_rows, tile_cols) + bias_b).astype(jnp.bfloat16)
    return (decoded, front[None])


def solution(mesh):
    in_specs = (
        P("slab", None, "tile", None),
        P("slab", None, "tile"),
        P("slab", None, None),
        P("slab", None),
        P("slab", None, None),
        P("slab", None),
        P("slab", None),
        P("slab"),
        P(),
        P(),
        P(),
        P(),
    )
    out_specs = (P("slab", "tile", None), P("slab", None, "tile"))
    return jax.shard_map(body, mesh=mesh, in_specs=in_specs, out_specs=out_specs, check_vma=False)
```

profile of v0, /device:TPU:1, one launch (start us, length us, event | category | flops | bytes accessed | tf_op | source)
XLA Modules:
  0.0 851.4 jit_solution(13505761106247215219)
XLA Ops:
  7.2 0.0 all-gather.3.cloned.1.call-start
  7.2 5.3 copy.24
  12.5 15.6 %fusion.32 = f32[256,16,4,256]{3,0,2,1:T(8,128)S(1)} fusion(f32[256,16,4,64]{0,3,2,1:T(8,128)} %bitcast.147, f32[1,64,256]{2,1,0:T(8,128)S(1)} %copy-done.4), kind=kOutput, calls=%fused_computation.42 | convolution fusion | flops 3221225472 | bytes 21037056 | tf_op jit(solution)/shard_map/rwkf,fh->rwkh/dot_general | solution.py:41
  28.1 5.7 copy-done.1
  33.8 15.2 %fusion.2 = f32[1,256,16,4]{0,1,3,2:T(8,128)} fusion(f32[256,16,4,256]{3,0,2,1:T(8,128)S(1)} %fusion.32, f32[256]{0:T(256)S(1)} %bitcast.153, f32[1,256]{1,0:T(1,128)S(1)} %copy-done.8), kind=kOutput, calls=%fused_computation.5 | convolution fusion | flops 58720256 | bytes 16844800 | tf_op jit(solution)/shard_map/rwkh,h->rwk/dot_general | solution.py:47
  49.1 5.2 copy.28
  55.0 0.7 fusion.111
  55.6 0.0 all-gather.3.cloned.1.call-update
  55.6 0.0 reduce-scatter.2.cloned.1.call-start
  55.7 296.8 %psum.7 = f32[256,16]{0,1:T(8,128)S(1)} all-reduce(f32[256,16]{0,1:T(8,128)} %fusion.111), channel_id=1, replica_groups=mesh['slab'=64,'tile'=2] {'slab'}, use_global_device_ids=true, to_apply=%region_3.4 | all-reduce | flops 4096 | bytes 32768 | tf_op jit(solution)/shard_map/psum | solution.py:111
  352.5 18.1 %broadcast_add_fusion = f32[256,16,4,128]{3,0,2,1:T(8,128)} fusion(f32[128]{0:T(128)S(1)} %bitcast.155, f32[256,16,4,256]{3,0,2,1:T(8,128)} %copy-done.1, f32[256]{0:T(256)S(1)} %bitcast.154, f32[1,256,128]{2,1,0:T(8,128)S(1)} %copy-done), kind=kOutput, calls=%fused_computation.12 | convolution fusion | flops 6452936704 | bytes 25298432 | tf_op jit(solution)/shard_map/rwkh,hc->rwkc/dot_general | solution.py:62
  370.6 1.5 copy.34
  372.1 0.6 divide_bitcast_fusion
  372.7 0.2 fusion.29
  372.9 1.1 copy.30
  374.1 35.2 %fusion.7 = f32[256,16,1,128]{3,2,1,0:T(1,128)} fusion(f32[256,16,4,1]{2,3,1,0:T(1,128)S(1)} %copy.30, f32[256,16,4,128]{3,0,2,1:T(8,128)} %broadcast_add_fusion), kind=kOutput, calls=%fused_computation.10 | convolution fusion | flops 25165824 | bytes 10551296 | tf_op jit(solution)/shard_map/rwk,rwkc->rwc/dot_general | solution.py:64
  409.3 356.2 %reduce-scatter.2.cloned.1.call-done = f32[4,16,128]{2,1,0:T(8,128)} async-done(((f32[256,16,128]{2,1,0:T(8,128)}), f32[4,16,128]{2,1,0:T(8,128)}) %reduce-scatter.2.cloned.1.call-update) | async-done | bytes 32784 | tf_op jit(solution)/shard_map/reduce_scatter | solution.py:114
  765.5 0.8 convert_element_type.9
  766.3 1.3 collective-permute-start
  767.6 1.3 collective-permute-start.1
  768.9 0.1 fusion.58
  769.0 3.3 collective-permute-done.1
  772.4 1.3 collective-permute-start.2
  773.7 56.3 %collective-permute-start.3 = (bf16[6,1,128]{2,1,0:T(2,128)(2,1)S(1)}, bf16[6,1,128]{2,1,0:T(2,128)(2,1)S(1)}, u32[]{:S(2)}, u32[]{:S(2)}) collective-permute-start(bf16[6,1,128]{2,1,0:T(2,128)(2,1)S(1)} %get-tuple-element.55), channel_id=1, source_target_pairs={{1,0},{3,2},{5,4},{7,6},{9,8},{11,10},{13,12},{15,14},{17,16},{19,... | collective-permute-start | bytes 4616 | tf_op jit(solution)/shard_map/ppermute | solution.py:20
  829.9 0.1 fusion.64
  830.1 0.1 fusion.53
  830.2 0.5 collective-permute-done.3
  830.8 0.1 fusion.62
  830.9 0.1 fusion.51
  831.0 0.1 fusion.60
  831.1 0.1 fusion.55
  831.3 0.1 fusion.26
  831.4 0.1 fusion.27
  831.6 1.4 collective-permute-start.4
  833.0 1.3 collective-permute-start.5
  834.3 0.1 fusion.42
  834.4 2.9 collective-permute-done.5
  837.3 1.3 collective-permute-start.6
  838.6 3.7 collective-permute-start.7
  842.3 0.1 fusion.48
  842.4 0.1 fusion.37
  842.6 0.5 collective-permute-done.7
  843.1 0.1 fusion.46
  843.3 0.1 fusion.35
  843.4 0.1 fusion.44
  843.5 0.1 fusion.39
  843.7 0.1 fusion.18
  843.8 0.8 fusion.28
  (35 shorter events, 0.2 us)
Async XLA Ops:
  7.2 345.3 %copy-start = (f32[1,256,128]{2,1,0:T(8,128)S(1)}, f32[1,256,128]{2,1,0:T(8,128)}, u32[]{:S(2)}) copy-start(f32[1,256,128]{2,1,0:T(8,128)} %param.18) | copy-start | bytes 393220
  7.2 5.3 copy-start.4
  7.2 363.4 %all-gather.3.cloned.1.call-start = ((), (), s32[]{:S(2)}) async-start(), calls=%async_computation.2 | async-start | bytes 1064960 | tf_op jit(solution)/shard_map/all_gather | solution.py:29
  12.5 21.3 %copy-start.6 = (f32[1,256]{1,0:T(1,128)S(1)}, f32[1,256]{1,0:T(1,128)}, u32[]{:S(2)}) copy-start(f32[1,256]{1,0:T(1,128)} %param.17) | copy-start | bytes 3076
  12.5 21.3 %copy-start.8 = (f32[1,256]{1,0:T(1,128)S(1)}, f32[1,256]{1,0:T(1,128)}, u32[]{:S(2)}) copy-start(f32[1,256]{1,0:T(1,128)} %param.20) | copy-start | bytes 3076
  28.1 5.7 copy-start.1
  49.1 5.9 copy-start.5
  49.1 303.4 %copy-start.7 = (f32[1,128]{1,0:T(1,128)S(1)}, f32[1,128]{1,0:T(1,128)}, u32[]{:S(2)}) copy-start(f32[1,128]{1,0:T(1,128)} %param.19) | copy-start | bytes 1540
  55.6 709.9 %reduce-scatter.2.cloned.1.call-start = ((), (), s32[]{:S(2)}) async-start(), calls=%async_computation.1 | async-start | bytes 2129920 | tf_op jit(solution)/shard_map/reduce_scatter | solution.py:114
  374.0 394.9 %copy-start.2 = (bf16[3,3,128,128]{3,2,1,0:T(8,128)(2,1)S(1)}, bf16[3,3,128,128]{3,2,1,0:T(8,128)(2,1)}, u32[]{:S(2)}) copy-start(bf16[3,3,128,128]{3,2,1,0:T(8,128)(2,1)} %param.22) | copy-start | bytes 884740
  374.0 457.4 %copy-start.9 = (f32[128]{0:T(128)S(1)}, f32[128]{0:T(128)}, u32[]{:S(2)}) copy-start(f32[128]{0:T(128)} %param.23) | copy-start | bytes 1540
  374.1 460.2 %copy-start.3 = (bf16[3,3,128,128]{3,2,1,0:T(8,128)(2,1)S(1)}, bf16[3,3,128,128]{3,2,1,0:T(8,128)(2,1)}, u32[]{:S(2)}) copy-start(bf16[3,3,128,128]{3,2,1,0:T(8,128)(2,1)} %param.24) | copy-start | bytes 884740
  374.1 469.7 %copy-start.10 = (f32[128]{0:T(128)S(1)}, f32[128]{0:T(128)}, u32[]{:S(2)}) copy-start(f32[128]{0:T(128)} %param.25) | copy-start | bytes 1540
  766.3 2.7 collective-permute-start
  767.6 4.8 collective-permute-start.1
  772.4 57.8 %collective-permute-start.2 = (bf16[6,1,128]{2,1,0:T(2,128)(2,1)S(1)}, bf16[6,1,128]{2,1,0:T(2,128)(2,1)S(1)}, u32[]{:S(2)}, u32[]{:S(2)}) collective-permute-start(bf16[6,1,128]{2,1,0:T(2,128)(2,1)S(1)} %get-tuple-element.54), channel_id=1, source_target_pairs={{0,1},{2,3},{4,5},{6,7},{8,9},{10,11},{12,13},{14,15},{16,17},{18,... | collective-permute-start | bytes 4616 | tf_op jit(solution)/shard_map/ppermute | solution.py:18
  773.7 57.1 %collective-permute-start.3 = (bf16[6,1,128]{2,1,0:T(2,128)(2,1)S(1)}, bf16[6,1,128]{2,1,0:T(2,128)(2,1)S(1)}, u32[]{:S(2)}, u32[]{:S(2)}) collective-permute-start(bf16[6,1,128]{2,1,0:T(2,128)(2,1)S(1)} %get-tuple-element.55), channel_id=1, source_target_pairs={{1,0},{3,2},{5,4},{7,6},{9,8},{11,10},{13,12},{15,14},{17,16},{19,... | collective-permute-start | bytes 4616 | tf_op jit(solution)/shard_map/ppermute | solution.py:20
  831.6 2.8 collective-permute-start.4
  833.0 4.4 collective-permute-start.5
  837.3 5.2 collective-permute-start.6
  838.6 4.5 collective-permute-start.7
Sparse Core Ops, SparseCore 0:
  55.8 64.9 all-gather.2
  409.4 356.0 reduce-scatter.1
where the time goes:
time: 852 us; the launch traced here: 851 us
  waiting for transfers between devices  364 us (43%)
  blocking collectives  297 us (35%)
  matrix products  87.1 us (10%)
  starting transfers between devices  67.8 us (8%)
  local copies, waits for them, and re-layouts  18.9 us (2%)
  between operations  14.9 us (2%)
    reduce_scatter x1, waiting for transfers between devices, body(): lax.psum_scatter(partial_image(hidden_act, weight, w_color[0], b_color[0]...  356 us
    psum x1, blocking collectives, body(): total = lax.psum(depth, 'slab')  297 us
    ppermute x4, starting transfers between devices, padded_2(): lax.ppermute(head, axis, [((i + 1) % count, i) for i in range(ends)])  62.5 us
    dot_general x1, matrix products, partial_image(): jnp.einsum('rwk,rwkc->rwc', weight, color, precision=lax.Precision.HIGHEST)  35.2 us
    dot_general x1, matrix products, partial_image(): jnp.einsum('rwkh,hc->rwkc', hidden_act, w_color, precision=lax.Precision....  18.1 us
  transfers between devices with their start and end apart: 10, of which 5 were waited for; matrix products, arithmetic and copies ran while one was open for 2% of the time, Pallas kernels for 0%

commit v1 on v0

--- a/solution.py
+++ b/solution.py
@@ -108,7 +108,7 @@
     density = densities(hidden_act, w_density[0], b_density[0], counts[0])
     depth = jnp.sum(density, axis=2)
     prefix = prefix_2(depth, "slab", add_pair, jnp.zeros_like(depth))
-    total = lax.psum(depth, "slab")
+    total = jnp.sum(lax.all_gather(depth, "slab"), axis=0)
     front = prefix / total
     weight = sample_weights(density, front, total)
     image = lax.psum_scatter(

time: 852 us -> 553 us (0.65)
  blocking collectives: 297 us -> 0 us
    psum x1 -> x0, blocking collectives: 297 us -> none  [body(): total = lax.psum(depth, 'slab')]
    reduce_scatter x1, waiting for transfers between devices: 356 us -> 308 us  [body(): lax.psum_scatter(partial_image(hidden_act, weight, w_color[0], b_color[0]...]
    all_gather x1, waiting for transfers between devices: 0.01 us -> 46.7 us  [prefix_2(): gathered = lax.all_gather(part, axis)]
  transfers between devices with their start and end apart: 10 -> 10, of which waited for: 5 -> 6; matrix products, arithmetic and copies ran while one was open for 2% -> 3% of each run, Pallas kernels for 0% -> 0%
where the time goes in v1:
time: 553 us
  waiting for transfers between devices  362 us (65%)
  matrix products  87.1 us (16%)
  starting transfers between devices  67.1 us (12%)
  local copies, waits for them, and re-layouts  18.9 us (3%)
  between operations  15 us (3%)
    reduce_scatter x1, waiting for transfers between devices, body(): lax.psum_scatter(partial_image(hidden_act, weight, w_color[0], b_color[0]...  308 us
    ppermute x4, starting transfers between devices, padded_2(): lax.ppermute(head, axis, [((i + 1) % count, i) for i in range(ends)])  61.6 us
    all_gather x1, waiting for transfers between devices, prefix_2(): gathered = lax.all_gather(part, axis)  46.7 us
    dot_general x1, matrix products, partial_image(): jnp.einsum('rwk,rwkc->rwc', weight, color, precision=lax.Precision.HIGHEST)  35.2 us
    dot_general x1, matrix products, partial_image(): jnp.einsum('rwkh,hc->rwkc', hidden_act, w_color, precision=lax.Precision....  18.1 us
    dot_general x1, matrix products, hidden_units(): jnp.einsum('rwkf,fh->rwkh', shaped, w_in, precision=lax.Precision.HIGHEST)  15.6 us
    dot_general x1, matrix products, densities(): jnp.einsum('rwkh,h->rwk', hidden_act, w_density, precision=lax.Precision....  15.2 us
    unnamed x24, local copies, waits for them, and re-layouts  12.6 us
  transfers between devices with their start and end apart: 10, of which 6 were waited for; matrix products, arithmetic and copies ran while one was open for 3% of the time, Pallas kernels for 0%

profile of v1, /device:TPU:1, one launch (start us, length us, event | category | flops | bytes accessed | tf_op | source)
XLA Modules:
  0.0 552.7 jit_solution(9292170776986317852)
XLA Ops:
  7.2 0.0 all-gather.3.cloned.1.call-start
  7.2 5.3 copy.23
  12.5 15.6 %fusion.32 = f32[256,16,4,256]{3,0,2,1:T(8,128)S(1)} fusion(f32[256,16,4,64]{0,3,2,1:T(8,128)} %bitcast.148, f32[1,64,256]{2,1,0:T(8,128)S(1)} %copy-done.4), kind=kOutput, calls=%fused_computation.42 | convolution fusion | flops 3221225472 | bytes 21037056 | tf_op jit(solution)/shard_map/rwkf,fh->rwkh/dot_general | solution.py:41
  28.1 5.7 %copy-done.1 = f32[256,16,4,256]{3,0,2,1:T(8,128)} copy-done((f32[256,16,4,256]{3,0,2,1:T(8,128)}, f32[256,16,4,256]{3,0,2,1:T(8,128)S(1)}, u32[]{:S(2)}) %copy-start.1) | copy-done | bytes 16777240
  33.8 15.2 %fusion.2 = f32[1,256,16,4]{0,1,3,2:T(8,128)} fusion(f32[256,16,4,256]{3,0,2,1:T(8,128)S(1)} %fusion.32, f32[256]{0:T(256)S(1)} %bitcast.154, f32[1,256]{1,0:T(1,128)S(1)} %copy-done.8), kind=kOutput, calls=%fused_computation.5 | convolution fusion | flops 58720256 | bytes 16844800 | tf_op jit(solution)/shard_map/rwkh,h->rwk/dot_general | solution.py:47
  49.1 5.2 copy.27
  55.0 0.7 fusion.111
  55.6 0.2 reduce-scatter.2.cloned.1.call-start
  55.9 18.1 %broadcast_add_fusion = f32[256,16,4,128]{3,0,2,1:T(8,128)} fusion(f32[128]{0:T(128)S(1)} %bitcast.156, f32[256,16,4,256]{3,0,2,1:T(8,128)} %copy-done.1, f32[256]{0:T(256)S(1)} %bitcast.155, f32[1,256,128]{2,1,0:T(8,128)S(1)} %copy-done), kind=kOutput, calls=%fused_computation.12 | convolution fusion | flops 6452936704 | bytes 25298432 | tf_op jit(solution)/shard_map/rwkh,hc->rwkc/dot_general | solution.py:62
  74.0 46.7 %all-gather.3.cloned.1.call-done = f32[16384,16]{0,1:T(8,128)} async-done(((f32[256,16]{0,1:T(8,128)}), f32[16384,16]{0,1:T(8,128)}) %all-gather.3.cloned.1.call-update) | async-done | bytes 1048592 | tf_op jit(solution)/shard_map/all_gather | solution.py:29
  120.7 1.5 copy.33
  122.3 0.1 bitcast_reduce_fusion
  122.4 0.6 divide_bitcast_fusion
  123.0 0.2 fusion.29
  123.2 1.1 copy.29
  124.3 35.2 %fusion.7 = f32[256,16,1,128]{3,2,1,0:T(1,128)} fusion(f32[256,16,4,1]{2,3,1,0:T(1,128)S(1)} %copy.29, f32[256,16,4,128]{3,0,2,1:T(8,128)} %broadcast_add_fusion), kind=kOutput, calls=%fused_computation.10 | convolution fusion | flops 25165824 | bytes 10551296 | tf_op jit(solution)/shard_map/rwk,rwkc->rwc/dot_general | solution.py:64
  159.6 308.1 %reduce-scatter.2.cloned.1.call-done = f32[4,16,128]{2,1,0:T(8,128)} async-done(((f32[256,16,128]{2,1,0:T(8,128)}), f32[4,16,128]{2,1,0:T(8,128)}) %reduce-scatter.2.cloned.1.call-update) | async-done | bytes 32784 | tf_op jit(solution)/shard_map/reduce_scatter | solution.py:114
  467.7 0.8 convert_element_type.9
  468.4 1.3 collective-permute-start
  469.7 1.3 collective-permute-start.1
  471.0 0.1 fusion.58
  471.2 3.3 collective-permute-done.1
  474.5 1.3 collective-permute-start.2
  475.8 55.4 %collective-permute-start.3 = (bf16[6,1,128]{2,1,0:T(2,128)(2,1)S(1)}, bf16[6,1,128]{2,1,0:T(2,128)(2,1)S(1)}, u32[]{:S(2)}, u32[]{:S(2)}) collective-permute-start(bf16[6,1,128]{2,1,0:T(2,128)(2,1)S(1)} %get-tuple-element.51), channel_id=1, source_target_pairs={{1,0},{3,2},{5,4},{7,6},{9,8},{11,10},{13,12},{15,14},{17,16},{19,... | collective-permute-start | bytes 4616 | tf_op jit(solution)/shard_map/ppermute | solution.py:20
  531.2 0.1 fusion.64
  531.3 0.1 fusion.53
  531.4 0.5 collective-permute-done.3
  532.0 0.1 fusion.62
  532.1 0.1 fusion.51
  532.3 0.1 fusion.60
  532.4 0.1 fusion.55
  532.5 0.1 fusion.26
  532.7 0.1 fusion.27
  532.9 1.4 collective-permute-start.4
  534.2 1.3 collective-permute-start.5
  535.5 0.1 fusion.42
  535.7 2.9 collective-permute-done.5
  538.6 1.3 collective-permute-start.6
  539.9 3.7 collective-permute-start.7
  543.6 0.1 fusion.48
  543.7 0.1 fusion.37
  543.8 0.5 collective-permute-done.7
  544.4 0.1 fusion.46
  544.5 0.1 fusion.35
  544.7 0.1 fusion.44
  544.8 0.1 fusion.39
  544.9 0.1 fusion.18
  545.1 0.8 fusion.28
  (35 shorter events, 0.2 us)
Async XLA Ops:
  7.2 48.7 %copy-start = (f32[1,256,128]{2,1,0:T(8,128)S(1)}, f32[1,256,128]{2,1,0:T(8,128)}, u32[]{:S(2)}) copy-start(f32[1,256,128]{2,1,0:T(8,128)} %param.18) | copy-start | bytes 393220
  7.2 5.3 copy-start.4
  7.2 113.6 %all-gather.3.cloned.1.call-start = ((), (), s32[]{:S(2)}) async-start(), calls=%async_computation.2 | async-start | bytes 1064960 | tf_op jit(solution)/shard_map/all_gather | solution.py:29
  12.5 21.3 %copy-start.6 = (f32[1,256]{1,0:T(1,128)S(1)}, f32[1,256]{1,0:T(1,128)}, u32[]{:S(2)}) copy-start(f32[1,256]{1,0:T(1,128)} %param.17) | copy-start | bytes 3076
  12.5 21.3 %copy-start.8 = (f32[1,256]{1,0:T(1,128)S(1)}, f32[1,256]{1,0:T(1,128)}, u32[]{:S(2)}) copy-start(f32[1,256]{1,0:T(1,128)} %param.20) | copy-start | bytes 3076
  28.1 5.7 %copy-start.1 = (f32[256,16,4,256]{3,0,2,1:T(8,128)}, f32[256,16,4,256]{3,0,2,1:T(8,128)S(1)}, u32[]{:S(2)}) copy-start(f32[256,16,4,256]{3,0,2,1:T(8,128)S(1)} %fusion.32) | copy-start | bytes 50331652
  49.1 5.9 %copy-start.5 = (s32[1,256,16]{1,2,0:T(8,128)S(1)}, s32[1,256,16]{1,2,0:T(8,128)}, u32[]{:S(2)}) copy-start(s32[1,256,16]{1,2,0:T(8,128)} %param.15) | copy-start | bytes 49156
  49.1 6.8 %copy-start.7 = (f32[1,128]{1,0:T(1,128)S(1)}, f32[1,128]{1,0:T(1,128)}, u32[]{:S(2)}) copy-start(f32[1,128]{1,0:T(1,128)} %param.19) | copy-start | bytes 1540
  55.6 412.0 %reduce-scatter.2.cloned.1.call-start = ((), (), s32[]{:S(2)}) async-start(), calls=%async_computation.1 | async-start | bytes 2129920 | tf_op jit(solution)/shard_map/reduce_scatter | solution.py:114
  124.3 346.7 %copy-start.2 = (bf16[3,3,128,128]{3,2,1,0:T(8,128)(2,1)S(1)}, bf16[3,3,128,128]{3,2,1,0:T(8,128)(2,1)}, u32[]{:S(2)}) copy-start(bf16[3,3,128,128]{3,2,1,0:T(8,128)(2,1)} %param.22) | copy-start | bytes 884740
  124.3 408.4 %copy-start.9 = (f32[128]{0:T(128)S(1)}, f32[128]{0:T(128)}, u32[]{:S(2)}) copy-start(f32[128]{0:T(128)} %param.23) | copy-start | bytes 1540
  124.3 411.2 %copy-start.3 = (bf16[3,3,128,128]{3,2,1,0:T(8,128)(2,1)S(1)}, bf16[3,3,128,128]{3,2,1,0:T(8,128)(2,1)}, u32[]{:S(2)}) copy-start(bf16[3,3,128,128]{3,2,1,0:T(8,128)(2,1)} %param.24) | copy-start | bytes 884740
  124.3 420.7 %copy-start.10 = (f32[128]{0:T(128)S(1)}, f32[128]{0:T(128)}, u32[]{:S(2)}) copy-start(f32[128]{0:T(128)} %param.25) | copy-start | bytes 1540
  468.4 2.7 collective-permute-start
  469.7 4.8 collective-permute-start.1
  474.5 57.0 %collective-permute-start.2 = (bf16[6,1,128]{2,1,0:T(2,128)(2,1)S(1)}, bf16[6,1,128]{2,1,0:T(2,128)(2,1)S(1)}, u32[]{:S(2)}, u32[]{:S(2)}) collective-permute-start(bf16[6,1,128]{2,1,0:T(2,128)(2,1)S(1)} %get-tuple-element.50), channel_id=1, source_target_pairs={{0,1},{2,3},{4,5},{6,7},{8,9},{10,11},{12,13},{14,15},{16,17},{18,... | collective-permute-start | bytes 4616 | tf_op jit(solution)/shard_map/ppermute | solution.py:18
  475.8 56.2 %collective-permute-start.3 = (bf16[6,1,128]{2,1,0:T(2,128)(2,1)S(1)}, bf16[6,1,128]{2,1,0:T(2,128)(2,1)S(1)}, u32[]{:S(2)}, u32[]{:S(2)}) collective-permute-start(bf16[6,1,128]{2,1,0:T(2,128)(2,1)S(1)} %get-tuple-element.51), channel_id=1, source_target_pairs={{1,0},{3,2},{5,4},{7,6},{9,8},{11,10},{13,12},{15,14},{17,16},{19,... | collective-permute-start | bytes 4616 | tf_op jit(solution)/shard_map/ppermute | solution.py:20
  532.9 2.8 collective-permute-start.4
  534.2 4.4 collective-permute-start.5
  538.6 5.2 collective-permute-start.6
  539.9 4.5 collective-permute-start.7
Sparse Core Ops, SparseCore 0:
  55.8 64.9 all-gather.2
  159.7 307.9 reduce-scatter.1
